TPU v7x, 32 devices: a whole 2x2x4 slice. The times are simulated.
32 devices in a mesh: member: 8 (over z, core), basin: 4 (over y, x).
Axes of the slice: x: 2, y: 2, z: 4, core: 2. Of those that a mesh axis runs over, the one named last changes fastest.
Arguments:
- prior_params: float32 [256, 8, 512], P('member', None, 'basin'), may hold values from -3 to 3
- lateral_flow: float32 [256, 2, 65536], P('member', None, 'basin'), may hold values from 0.2 to 2
- inflow_start: float32 [65536], P('basin'), may hold values from 0.5 to 4
- outflow_start: float32 [65536], P('basin'), may hold values from 0.5 to 4
- reach_count: int32 [512], P('basin'), may hold values from 64 to 128
- downstream: int32 [512], P('basin'), may hold values from 0 to 63
- gauge_reach: int32 [2048], P('basin'), may hold values from 0 to 16383
- observed: float32 [2, 2048], P(None, 'basin'), may hold values from 0.5 to 4
- obs_var: float32 [2, 2048], P(None, 'basin'), may hold values from 0.02 to 0.5
- obs_noise: float32 [256, 2, 2048], P('member', None, 'basin'), may hold values from -4 to 4
Outputs:
- posterior: float32 [256, 8, 512], P('member', None, 'basin')
- predicted: float32 [256, 2, 2048], P('member', None, 'basin')
All inputs are finite; a program needn't handle non-finite values.
Results may differ from a plain program's by a relative error of at most 0.0003.
Values sent between devices are 32-bit elements; how exact they have to be, the bound alone decides.
A program may use at most 128 MiB of HBM per device.

v0:
```python
import math
import jax
import jax.numpy as jnp
from jax import lax
from jax.sharding import PartitionSpec as P

LANES = 128
BLK_LEV = 64
exact_mode = lax.Precision.HIGHEST


def shifted(block, axis, distance):
    devices = range(lax.axis_size(axis))
    route = [(i - distance, i) for i in devices if i - distance in devices]
    return lax.ppermute(block, axis, route)


def inverse_sinh(values):
    return jnp.log(values + jnp.sqrt(values * values + 1.0))


def route_coefficients(prior_params):
    storage = 0.02 + 0.1 * jax.nn.sigmoid(prior_params[:, 0, :])
    weighting = 0.2 * jax.nn.sigmoid(prior_params[:, 1, :])
    denominator = storage * (1.0 - weighting) + 0.5
    weight_now = (0.5 - storage * weighting) / denominator
    weight_back = (0.5 + storage * weighting) / denominator
    weight_carry = (storage * (1.0 - weighting) - 0.5) / denominator
    return (weight_now[:, :, None], weight_back[:, :, None], weight_carry[:, :, None])


def lateral_scaling(prior_params, lane_count):
    lane_pos = jnp.arange(lane_count, dtype=jnp.float32)
    orders = jnp.arange(6, dtype=jnp.float32)
    cosine_modes = jnp.cos(math.pi * orders[:, None] * (lane_pos[None, :] + 0.5) / lane_count)
    exponent = jnp.einsum(
        "mkb,kr->mbr", 0.2 * prior_params[:, 2:, :], cosine_modes, precision=exact_mode
    )
    return jnp.exp(exponent)


def solve_gram(gram_matrix, cross_matrix):
    factor = jnp.linalg.cholesky(gram_matrix)
    halfway = lax.linalg.triangular_solve(factor, cross_matrix, left_side=True, lower=True)
    return lax.linalg.triangular_solve(
        factor, halfway, left_side=True, lower=True, transpose_a=True
    )


def level_sweep(incoming, weights, lateral_now, live_mask, one_hot, prev_in, prev_out):
    weight_now, weight_back, weight_carry, scaling = weights
    level_blocks = one_hot[0].shape[0]
    upstream = incoming
    inflows = []
    outflows = []
    for level_idx in range(len(one_hot)):
        level_span = slice(level_idx * level_blocks, (level_idx + 1) * level_blocks)
        inflow = live_mask[level_span] * (
            lateral_now[:, level_span] * scaling[:, level_span] + upstream
        )
        outflow = (
            weight_now[:, level_span] * inflow
            + weight_back[:, level_span] * prev_in[:, level_span]
            + weight_carry[:, level_span] * prev_out[:, level_span]
        )
        upstream = jnp.einsum("nj,gjr->gnr", one_hot[level_idx], outflow, precision=exact_mode)
        inflows.append(inflow)
        outflows.append(outflow)
    return (jnp.concatenate(inflows, 1), jnp.concatenate(outflows, 1), upstream)


def route_hour(mover, groups, weights, lateral_now, live_mask, one_hot, prev_in, prev_out):
    members_dev, block_dev, lane_count = prev_in.shape
    level_blocks = one_hot[0].shape[0]
    group_size = members_dev // groups
    basins = lax.axis_size("basin")
    basin_idx = lax.axis_index("basin")

    def advance(step_idx, state_tuple):
        incoming, inflow_all, outflow_all = state_tuple
        group_idx = step_idx - basin_idx
        active = (group_idx >= 0) & (group_idx < groups)
        first_row = jnp.clip(group_idx, 0, groups - 1) * group_size

        def compute(operands):
            arriving, inflow_keep, outflow_keep = operands

            def take_group(values):
                return lax.dynamic_slice_in_dim(values, first_row, group_size, 0)

            group_weights = tuple((take_group(item) for item in weights))
            inflow, outflow, passed = level_sweep(
                arriving,
                group_weights,
                take_group(lateral_now),
                live_mask,
                one_hot,
                take_group(prev_in),
                take_group(prev_out),
            )
            inflow_keep = lax.dynamic_update_slice_in_dim(inflow_keep, inflow, first_row, 0)
            outflow_keep = lax.dynamic_update_slice_in_dim(outflow_keep, outflow, first_row, 0)
            return (passed, inflow_keep, outflow_keep)

        def skipped(operands):
            return (jnp.zeros_like(operands[0]), operands[1], operands[2])

        passed, inflow_all, outflow_all = lax.cond(
            active, compute, skipped, (incoming, inflow_all, outflow_all)
        )
        return (mover(passed), inflow_all, outflow_all)

    initial = (
        jnp.zeros((group_size, level_blocks, lane_count), jnp.float32),
        jnp.zeros_like(prev_in),
        jnp.zeros_like(prev_out),
    )
    _, inflow_all, outflow_all = lax.fori_loop(0, basins + groups - 1, advance, initial)
    return (inflow_all, outflow_all)


def shards(
    prior_params,
    lateral_flow,
    inflow_start,
    outflow_start,
    reach_count,
    downstream,
    gauge_reach,
    observed,
    obs_var,
    obs_noise,
):
    members_dev, param_count, block_dev = prior_params.shape
    lane_count = LANES
    level_blocks = BLK_LEV
    level_count = block_dev // level_blocks
    hour_count = lateral_flow.shape[1]
    lane_ids = jnp.arange(lane_count, dtype=jnp.int32)
    live_mask = (lane_ids[None, :] < reach_count[:, None]).astype(jnp.float32)
    targets = jnp.arange(level_blocks, dtype=jnp.int32)
    one_hot = [
        (
            downstream[None, level_idx * level_blocks : (level_idx + 1) * level_blocks]
            == targets[:, None]
        ).astype(jnp.float32)
        for level_idx in range(level_count)
    ]
    weight_now, weight_back, weight_carry = route_coefficients(prior_params)
    scaling = lateral_scaling(prior_params, lane_count)
    weights = (weight_now, weight_back, weight_carry, scaling)
    lateral_grid = lateral_flow.reshape(members_dev, hour_count, block_dev, lane_count)
    prev_in = jnp.broadcast_to(
        (inflow_start.reshape(block_dev, lane_count) * live_mask)[None],
        (members_dev, block_dev, lane_count),
    )
    prev_out = jnp.broadcast_to(
        (outflow_start.reshape(block_dev, lane_count) * live_mask)[None],
        (members_dev, block_dev, lane_count),
    )
    results = []
    for hour_idx in range(hour_count):
        lateral_now = lateral_grid[:, hour_idx]
        prev_in, prev_out = route_hour(
            lambda passed: shifted(passed, "basin", 1),
            4,
            weights,
            lateral_now,
            live_mask,
            one_hot,
            prev_in,
            prev_out,
        )
        flat = prev_out.reshape(members_dev, block_dev * lane_count)
        results.append(inverse_sinh(jnp.take(flat, gauge_reach, axis=1)))
    predicted = jnp.stack(results, 1)
    members = members_dev * lax.axis_size("member")
    spread = jnp.sqrt(obs_var)
    spread_root = math.sqrt(members - 1.0)
    innovation = (observed + 2.0 * spread * obs_noise - predicted) / (2.0 * spread)
    mean_pred = lax.psum(jnp.sum(predicted, 0), "member") / members
    scaled = (predicted - mean_pred) / (spread_root * (2.0 * spread))
    scaled_all, innov_all = (
        lax.all_gather(scaled, "member", axis=0, tiled=True),
        lax.all_gather(innovation, "member", axis=0, tiled=True),
    )
    scaled_rows = scaled_all.reshape(members, -1)
    innov_rows = innov_all.reshape(members, -1)
    gram_part = jnp.dot(
        scaled_rows, scaled_rows.T, precision=exact_mode, preferred_element_type=jnp.float32
    )
    cross_part = jnp.dot(
        scaled_rows, innov_rows.T, precision=exact_mode, preferred_element_type=jnp.float32
    )
    gram_matrix, cross_matrix = lax.psum((gram_part, cross_part), "basin")
    gram_matrix = gram_matrix + jnp.eye(members, dtype=jnp.float32)
    solved = solve_gram(gram_matrix, cross_matrix)
    prior_all = lax.all_gather(prior_params, "member", axis=0, tiled=True)
    mean_prior = jnp.sum(prior_all, 0) / members
    anomaly = (prior_all - mean_prior) / spread_root
    own_cols = lax.dynamic_slice_in_dim(
        solved, lax.axis_index("member") * members_dev, members_dev, 1
    )
    posterior = prior_params + jnp.einsum("mn,mkb->nkb", own_cols, anomaly, precision=exact_mode)
    return (posterior, predicted)


def solution(mesh):
    return jax.shard_map(
        shards,
        mesh=mesh,
        in_specs=(
            P("member", None, "basin"),
            P("member", None, "basin"),
            P("basin"),
            P("basin"),
            P("basin"),
            P("basin"),
            P("basin"),
            P(None, "basin"),
            P(None, "basin"),
            P("member", None, "basin"),
        ),
        out_specs=(P("member", None, "basin"), P("member", None, "basin")),
        check_vma=False,
    )
```

profile of v0, /device:TPU:0, one launch (start us, length us, event | category | flops | bytes accessed | tf_op | source)
XLA Modules:
  0.0 468.4 jit_solution(3943242846933802712)
XLA Ops:
  12.6 6.6 %reshape.277 = f32[32,2,128,128]{3,2,1,0:T(8,128)} reshape(f32[32,2,16384]{2,1,0:T(2,128)} %param.21) | data formatting | bytes 8388608 | tf_op jit(solution)/shard_map/reshape | solution.py:152
  19.2 4.9 %slice_bitcast_fusion.13 = (f32[32,128,128]{2,1,0:T(8,128)}, f32[32,128,128]{2,1,0:T(8,128)}) fusion(f32[32,2,128,128]{3,2,1,0:T(8,128)} %reshape.277), kind=kLoop, calls=%fused_computation.78 | loop fusion | bytes 8388608 | tf_op jit(solution)/shard_map/squeeze | solution.py:163
  24.1 3.5 convolution_exponential_fusion
  28.3 1.6 broadcast.366.clone
  30.0 1.5 broadcast.366.clone.1
  31.5 106.7 %while.39 = (s32[]{:T(128)}, f32[8,64,128]{2,1,0:T(8,128)S(1)}, f32[32,128,128]{2,1,0:T(8,128)}, f32[32,128,128]{2,1,0:T(8,128)}, s32[]{:T(128)}, /*index=5*/f32...) while((s32[]{:T(128)}, f32[8,64,128]{2,1,0:T(8,128)S(1)}, ...), condition=%wide.region_3.4_spmd.clone, body=%wide.region_0.3_spmd.clone.sunk | while | flops 102023184 | bytes 7075321 | solution.py:118
  33.0 5.8 %conditional.6 = (f32[8,64,128]{2,1,0:T(8,128)S(1)}, f32[32,128,128]{2,1,0:T(8,128)}, f32[32,128,128]{2,1,0:T(8,128)}) conditional(s32[]{:T(128)} %convert_element_type.73, (f32[32,128,128]{2,1,0:T(8,128)}, f32[32,128,128]{2,1,0:T(8,128)}) %tuple.149, (s32[]{:T(128)}, f32[32,128,1]{1,0,2:T(8,128)S(1)}, f32[128,128]{1,0:T(8,128)S(1)}, ...), branch_computations={%region_1.1_spmd, %region_2.2_spmd} | conditional | flops 101974024 | bytes 5927046 | solution.py:108
  40.1 6.5 %collective-permute-done = f32[8,64,128]{2,1,0:T(8,128)S(1)} collective-permute-done((f32[8,64,128]{2,1,0:T(8,128)S(1)}, f32[8,64,128]{2,1,0:T(8,128)S(1)}, u32[]{:S(2)}, u32[]{:S(2)}) %collective-permute-start) | collective-permute-done | bytes 262176 | tf_op jit(solution)/shard_map/while/body/eval_jaxpr/ppermute | solution.py:15
  47.9 5.7 %conditional.6 = (f32[8,64,128]{2,1,0:T(8,128)S(1)}, f32[32,128,128]{2,1,0:T(8,128)}, f32[32,128,128]{2,1,0:T(8,128)}) conditional(s32[]{:T(128)} %convert_element_type.73, (f32[32,128,128]{2,1,0:T(8,128)}, f32[32,128,128]{2,1,0:T(8,128)}) %tuple.149, (s32[]{:T(128)}, f32[32,128,1]{1,0,2:T(8,128)S(1)}, f32[128,128]{1,0:T(8,128)S(1)}, ...), branch_computations={%region_1.1_spmd, %region_2.2_spmd} | conditional | flops 101974024 | bytes 5927046 | solution.py:108
  50.9 1.4 multiply_add_fusion
  53.7 4.4 collective-permute-start
  58.1 5.6 %collective-permute-done = f32[8,64,128]{2,1,0:T(8,128)S(1)} collective-permute-done((f32[8,64,128]{2,1,0:T(8,128)S(1)}, f32[8,64,128]{2,1,0:T(8,128)S(1)}, u32[]{:S(2)}, u32[]{:S(2)}) %collective-permute-start) | collective-permute-done | bytes 262176 | tf_op jit(solution)/shard_map/while/body/eval_jaxpr/ppermute | solution.py:15
  65.2 5.8 %conditional.6 = (f32[8,64,128]{2,1,0:T(8,128)S(1)}, f32[32,128,128]{2,1,0:T(8,128)}, f32[32,128,128]{2,1,0:T(8,128)}) conditional(s32[]{:T(128)} %convert_element_type.73, (f32[32,128,128]{2,1,0:T(8,128)}, f32[32,128,128]{2,1,0:T(8,128)}) %tuple.149, (s32[]{:T(128)}, f32[32,128,1]{1,0,2:T(8,128)S(1)}, f32[128,128]{1,0:T(8,128)S(1)}, ...), branch_computations={%region_1.1_spmd, %region_2.2_spmd} | conditional | flops 101974024 | bytes 5927046 | solution.py:108
  70.9 4.4 collective-permute-start
  75.3 4.8 %collective-permute-done = f32[8,64,128]{2,1,0:T(8,128)S(1)} collective-permute-done((f32[8,64,128]{2,1,0:T(8,128)S(1)}, f32[8,64,128]{2,1,0:T(8,128)S(1)}, u32[]{:S(2)}, u32[]{:S(2)}) %collective-permute-start) | collective-permute-done | bytes 262176 | tf_op jit(solution)/shard_map/while/body/eval_jaxpr/ppermute | solution.py:15
  81.5 5.8 %conditional.6 = (f32[8,64,128]{2,1,0:T(8,128)S(1)}, f32[32,128,128]{2,1,0:T(8,128)}, f32[32,128,128]{2,1,0:T(8,128)}) conditional(s32[]{:T(128)} %convert_element_type.73, (f32[32,128,128]{2,1,0:T(8,128)}, f32[32,128,128]{2,1,0:T(8,128)}) %tuple.149, (s32[]{:T(128)}, f32[32,128,1]{1,0,2:T(8,128)S(1)}, f32[128,128]{1,0:T(8,128)S(1)}, ...), branch_computations={%region_1.1_spmd, %region_2.2_spmd} | conditional | flops 101974024 | bytes 5927046 | solution.py:108
  87.3 4.4 collective-permute-start
  91.7 3.9 collective-permute-done
  97.1 10.3 %collective-permute-start = (f32[8,64,128]{2,1,0:T(8,128)S(1)}, f32[8,64,128]{2,1,0:T(8,128)S(1)}, u32[]{:S(2)}, u32[]{:S(2)}) collective-permute-start(f32[8,64,128]{2,1,0:T(8,128)S(1)} %get-tuple-element.1072), channel_id=1, source_target_pairs={{0,1},{1,2},{2,3},{4,5},{5,6},{6,7},{8,9},{9,10},{10,11},{12,13},{... | collective-permute-start | bytes 786440 | tf_op jit(solution)/shard_map/while/body/eval_jaxpr/ppermute | solution.py:15
  107.4 3.9 collective-permute-done
  112.7 5.3 %collective-permute-start = (f32[8,64,128]{2,1,0:T(8,128)S(1)}, f32[8,64,128]{2,1,0:T(8,128)S(1)}, u32[]{:S(2)}, u32[]{:S(2)}) collective-permute-start(f32[8,64,128]{2,1,0:T(8,128)S(1)} %get-tuple-element.1072), channel_id=1, source_target_pairs={{0,1},{1,2},{2,3},{4,5},{5,6},{6,7},{8,9},{9,10},{10,11},{12,13},{... | collective-permute-start | bytes 786440 | tf_op jit(solution)/shard_map/while/body/eval_jaxpr/ppermute | solution.py:15
  118.0 3.9 collective-permute-done
  123.4 11.0 %collective-permute-start = (f32[8,64,128]{2,1,0:T(8,128)S(1)}, f32[8,64,128]{2,1,0:T(8,128)S(1)}, u32[]{:S(2)}, u32[]{:S(2)}) collective-permute-start(f32[8,64,128]{2,1,0:T(8,128)S(1)} %get-tuple-element.1072), channel_id=1, source_target_pairs={{0,1},{1,2},{2,3},{4,5},{5,6},{6,7},{8,9},{9,10},{10,11},{12,13},{... | collective-permute-start | bytes 786440 | tf_op jit(solution)/shard_map/while/body/eval_jaxpr/ppermute | solution.py:15
  134.4 3.9 collective-permute-done
  138.2 6.4 %copy.30 = f32[32,128,128]{0,2,1:T(8,128)} copy(f32[32,128,128]{2,1,0:T(8,128)} %get-tuple-element.1167) | data formatting | bytes 4194304 | tf_op jit(solution)/shard_map/while | solution.py:118
  144.6 1.6 broadcast.366
  146.2 98.9 %while.40 = (s32[]{:T(128)}, f32[8,64,128]{2,1,0:T(8,128)S(1)}, f32[32,128,128]{2,1,0:T(8,128)}, s32[]{:T(128)}, f32[32,128,1]{1,0,2:T(8,128)S(1)}, /*index=5*/f...) while((s32[]{:T(128)}, f32[8,64,128]{2,1,0:T(8,128)S(1)}, ...), condition=%wide.region_7.9_spmd.clone, body=%wide.region_4.8_spmd.clone.sunk | while | flops 101892112 | bytes 6157773 | solution.py:118
  147.7 5.1 %conditional.7 = (f32[8,64,128]{2,1,0:T(8,128)S(1)}, f32[32,128,128]{2,1,0:T(8,128)}) conditional(s32[]{:T(128)} %convert_element_type.76, f32[32,128,128]{2,1,0:T(8,128)} %get-tuple-element.1176, (s32[]{:T(128)}, f32[32,128,1]{1,0,2:T(8,128)S(1)}, f32[128,128]{1,0:T(8,128)S(1)}, f32[32,128,128]{2,1,0:T(8,128)}, f32[32,128,128]{2,1,0:T(8,128)S(1)}, ...), branch_computations={%region_5.6_spmd, %region_6.7_spmd} | conditional | flops 101842952 | bytes 5009530 | solution.py:108
  150.0 1.6 fusion.26
  154.1 3.9 collective-permute-done.1
  159.4 5.1 %conditional.7 = (f32[8,64,128]{2,1,0:T(8,128)S(1)}, f32[32,128,128]{2,1,0:T(8,128)}) conditional(s32[]{:T(128)} %convert_element_type.76, f32[32,128,128]{2,1,0:T(8,128)} %get-tuple-element.1176, (s32[]{:T(128)}, f32[32,128,1]{1,0,2:T(8,128)S(1)}, f32[128,128]{1,0:T(8,128)S(1)}, f32[32,128,128]{2,1,0:T(8,128)}, f32[32,128,128]{2,1,0:T(8,128)S(1)}, ...), branch_computations={%region_5.6_spmd, %region_6.7_spmd} | conditional | flops 101842952 | bytes 5009530 | solution.py:108
  161.8 1.6 fusion.26
  164.5 5.7 %collective-permute-start.1 = (f32[8,64,128]{2,1,0:T(8,128)S(1)}, f32[8,64,128]{2,1,0:T(8,128)S(1)}, u32[]{:S(2)}, u32[]{:S(2)}) collective-permute-start(f32[8,64,128]{2,1,0:T(8,128)S(1)} %get-tuple-element.1091), channel_id=1, source_target_pairs={{0,1},{1,2},{2,3},{4,5},{5,6},{6,7},{8,9},{9,10},{10,11},{12,13},{... | collective-permute-start | bytes 786440 | tf_op jit(solution)/shard_map/while/body/eval_jaxpr/ppermute | solution.py:15
  170.2 3.9 collective-permute-done.1
  175.5 5.1 %conditional.7 = (f32[8,64,128]{2,1,0:T(8,128)S(1)}, f32[32,128,128]{2,1,0:T(8,128)}) conditional(s32[]{:T(128)} %convert_element_type.76, f32[32,128,128]{2,1,0:T(8,128)} %get-tuple-element.1176, (s32[]{:T(128)}, f32[32,128,1]{1,0,2:T(8,128)S(1)}, f32[128,128]{1,0:T(8,128)S(1)}, f32[32,128,128]{2,1,0:T(8,128)}, f32[32,128,128]{2,1,0:T(8,128)S(1)}, ...), branch_computations={%region_5.6_spmd, %region_6.7_spmd} | conditional | flops 101842952 | bytes 5009530 | solution.py:108
  177.8 1.6 fusion.26
  180.6 4.4 collective-permute-start.1
  185.1 3.9 collective-permute-done.1
  190.3 5.1 %conditional.7 = (f32[8,64,128]{2,1,0:T(8,128)S(1)}, f32[32,128,128]{2,1,0:T(8,128)}) conditional(s32[]{:T(128)} %convert_element_type.76, f32[32,128,128]{2,1,0:T(8,128)} %get-tuple-element.1176, (s32[]{:T(128)}, f32[32,128,1]{1,0,2:T(8,128)S(1)}, f32[128,128]{1,0:T(8,128)S(1)}, f32[32,128,128]{2,1,0:T(8,128)}, f32[32,128,128]{2,1,0:T(8,128)S(1)}, ...), branch_computations={%region_5.6_spmd, %region_6.7_spmd} | conditional | flops 101842952 | bytes 5009530 | solution.py:108
  192.7 1.6 fusion.26
  195.5 4.4 collective-permute-start.1
  199.9 3.9 collective-permute-done.1
  205.2 9.5 %collective-permute-start.1 = (f32[8,64,128]{2,1,0:T(8,128)S(1)}, f32[8,64,128]{2,1,0:T(8,128)S(1)}, u32[]{:S(2)}, u32[]{:S(2)}) collective-permute-start(f32[8,64,128]{2,1,0:T(8,128)S(1)} %get-tuple-element.1091), channel_id=1, source_target_pairs={{0,1},{1,2},{2,3},{4,5},{5,6},{6,7},{8,9},{9,10},{10,11},{12,13},{... | collective-permute-start | bytes 786440 | tf_op jit(solution)/shard_map/while/body/eval_jaxpr/ppermute | solution.py:15
  214.7 5.5 %collective-permute-done.1 = f32[8,64,128]{2,1,0:T(8,128)S(1)} collective-permute-done((f32[8,64,128]{2,1,0:T(8,128)S(1)}, f32[8,64,128]{2,1,0:T(8,128)S(1)}, u32[]{:S(2)}, u32[]{:S(2)}) %collective-permute-start.1) | collective-permute-done | bytes 262176 | tf_op jit(solution)/shard_map/while/body/eval_jaxpr/ppermute | solution.py:15
  221.7 4.4 collective-permute-start.1
  226.1 4.6 collective-permute-done.1
  232.2 9.1 %collective-permute-start.1 = (f32[8,64,128]{2,1,0:T(8,128)S(1)}, f32[8,64,128]{2,1,0:T(8,128)S(1)}, u32[]{:S(2)}, u32[]{:S(2)}) collective-permute-start(f32[8,64,128]{2,1,0:T(8,128)S(1)} %get-tuple-element.1091), channel_id=1, source_target_pairs={{0,1},{1,2},{2,3},{4,5},{5,6},{6,7},{8,9},{9,10},{10,11},{12,13},{... | collective-permute-start | bytes 786440 | tf_op jit(solution)/shard_map/while/body/eval_jaxpr/ppermute | solution.py:15
  241.3 3.9 collective-permute-done.1
  245.2 6.3 %copy.32 = f32[32,128,128]{0,2,1:T(8,128)} copy(f32[32,128,128]{2,1,0:T(8,128)} %get-tuple-element.648) | data formatting | bytes 4194304 | tf_op jit(solution)/shard_map/while | solution.py:118
  251.5 4.4 gather_fusion.1
  256.0 4.4 gather_fusion
  261.4 13.6 %psum.21 = f32[2,512]{1,0:T(2,128)S(1)} all-reduce(f32[2,512]{1,0:T(2,128)S(1)} %get-tuple-element.849), channel_id=1, replica_groups=mesh['member'=8,'basin'=4] {'member'}, use_global_device_ids=true, to_apply=%region_9.11 | all-reduce | flops 1024 | bytes 8192 | tf_op jit(solution)/shard_map/psum | solution.py:181
  277.4 23.8 %all-gather.4.cloned.1.call-done = f32[256,2,512]{2,0,1:T(8,128)} async-done(((f32[32,2,512]{2,0,1:T(8,128)}), f32[256,2,512]{2,0,1:T(8,128)}) %all-gather.4.cloned.1.call-update) | async-done | bytes 1048592 | tf_op jit(solution)/shard_map/all_gather | solution.py:184
  301.2 3.3 convolution_bitcast_fusion.5
  304.5 20.7 %all-gather.6.cloned.1.call-done = f32[256,2,512]{2,0,1:T(8,128)} async-done(((f32[32,2,512]{2,0,1:T(8,128)}), f32[256,2,512]{2,0,1:T(8,128)}) %all-gather.6.cloned.1.call-update) | async-done | bytes 1048592 | tf_op jit(solution)/shard_map/all_gather | solution.py:185
  325.2 3.0 convolution_bitcast_fusion.4
  329.0 19.7 %all-gather.8.cloned.1.call-done = f32[256,8,128]{2,1,0:T(8,128)} async-done(((f32[32,8,128]{2,1,0:T(8,128)}), f32[256,8,128]{2,1,0:T(8,128)}) %all-gather.8.cloned.1.call-update) | async-done | bytes 1048592 | tf_op jit(solution)/shard_map/all_gather | solution.py:198
  348.7 1.5 reduce_sum.19
  351.5 45.1 %all-reduce.4.cloned.1.call-done = (f32[256,256]{1,0:T(8,128)}, f32[256,256]{0,1:T(8,128)}) async-done(((f32[256,256]{1,0:T(8,128)}, f32[256,256]{0,1:T(8,128)}), (f32[256,256]{1,0:T(8,128)}, f32[256,256]{0,1:T(8,128)})) %all-reduce.4.cloned.1.call-update) | async-done | bytes 524304 | tf_op jit(solution)/shard_map/psum | solution.py:195
  398.7 11.7 %cholesky.49 = f32[128,128]{1,0:T(8,128)S(1)} custom-call(f32[128,128]{1,0:T(8,128)S(1)} %cholesky.115), custom_call_target="Cholesky" | custom-call | tf_op jit(solution)/shard_map/jit(cholesky)/cholesky | solution.py:43
  410.5 9.8 %custom-call.16 = f32[1,128,128]{1,2,0:T(8,128)S(1)} custom-call(f32[1,128,128]{2,1,0:T(8,128)S(1)} %get-tuple-element.857), custom_call_target="InvertDiagBlocksLowerTriangular" | custom-call | tf_op jit(solution)/shard_map/jit(cholesky)/cholesky | solution.py:43
  420.8 11.9 %cholesky.102 = f32[128,128]{1,0:T(8,128)S(1)} custom-call(f32[128,128]{1,0:T(8,128)S(1)} %convolution_subtract_fusion.2), custom_call_target="Cholesky" | custom-call | tf_op jit(solution)/shard_map/jit(cholesky)/cholesky | solution.py:43
  434.8 3.9 while.38
  438.7 19.7 %custom-call.17 = f32[2,128,128]{1,2,0:T(8,128)S(1)} custom-call(f32[2,128,128]{2,1,0:T(8,128)S(1)} %get-tuple-element.656), custom_call_target="InvertDiagBlocksLowerTriangular" | custom-call | tf_op jit(solution)/shard_map/triangular_solve | solution.py:45
  (208 shorter events, 80.4 us)
Async XLA Ops:
  7.2 294.0 %all-gather.4.cloned.1.call-start = ((), (), s32[]{:S(2)}) async-start(), calls=%async_computation | async-start | bytes 1179648 | tf_op jit(solution)/shard_map/all_gather | solution.py:184
  19.2 4.9 %copy-start.1 = (f32[32,8,128]{2,1,0:T(8,128)S(1)}, f32[32,8,128]{2,1,0:T(8,128)}, u32[]{:S(2)}) copy-start(f32[32,8,128]{2,1,0:T(8,128)} %param.20) | copy-start | bytes 393220
  24.1 3.5 copy-start.5
  24.1 3.5 copy-start.6
  38.7 7.8 %collective-permute-start = (f32[8,64,128]{2,1,0:T(8,128)S(1)}, f32[8,64,128]{2,1,0:T(8,128)S(1)}, u32[]{:S(2)}, u32[]{:S(2)}) collective-permute-start(f32[8,64,128]{2,1,0:T(8,128)S(1)} %get-tuple-element.1072), channel_id=1, source_target_pairs={{0,1},{1,2},{2,3},{4,5},{5,6},{6,7},{8,9},{9,10},{10,11},{12,13},{... | collective-permute-start | bytes 786440 | tf_op jit(solution)/shard_map/while/body/eval_jaxpr/ppermute | solution.py:15
  53.7 10.0 %collective-permute-start = (f32[8,64,128]{2,1,0:T(8,128)S(1)}, f32[8,64,128]{2,1,0:T(8,128)S(1)}, u32[]{:S(2)}, u32[]{:S(2)}) collective-permute-start(f32[8,64,128]{2,1,0:T(8,128)S(1)} %get-tuple-element.1072), channel_id=1, source_target_pairs={{0,1},{1,2},{2,3},{4,5},{5,6},{6,7},{8,9},{9,10},{10,11},{12,13},{... | collective-permute-start | bytes 786440 | tf_op jit(solution)/shard_map/while/body/eval_jaxpr/ppermute | solution.py:15
  70.9 9.2 %collective-permute-start = (f32[8,64,128]{2,1,0:T(8,128)S(1)}, f32[8,64,128]{2,1,0:T(8,128)S(1)}, u32[]{:S(2)}, u32[]{:S(2)}) collective-permute-start(f32[8,64,128]{2,1,0:T(8,128)S(1)} %get-tuple-element.1072), channel_id=1, source_target_pairs={{0,1},{1,2},{2,3},{4,5},{5,6},{6,7},{8,9},{9,10},{10,11},{12,13},{... | collective-permute-start | bytes 786440 | tf_op jit(solution)/shard_map/while/body/eval_jaxpr/ppermute | solution.py:15
  87.3 8.3 %collective-permute-start = (f32[8,64,128]{2,1,0:T(8,128)S(1)}, f32[8,64,128]{2,1,0:T(8,128)S(1)}, u32[]{:S(2)}, u32[]{:S(2)}) collective-permute-start(f32[8,64,128]{2,1,0:T(8,128)S(1)} %get-tuple-element.1072), channel_id=1, source_target_pairs={{0,1},{1,2},{2,3},{4,5},{5,6},{6,7},{8,9},{9,10},{10,11},{12,13},{... | collective-permute-start | bytes 786440 | tf_op jit(solution)/shard_map/while/body/eval_jaxpr/ppermute | solution.py:15
  97.1 14.2 %collective-permute-start = (f32[8,64,128]{2,1,0:T(8,128)S(1)}, f32[8,64,128]{2,1,0:T(8,128)S(1)}, u32[]{:S(2)}, u32[]{:S(2)}) collective-permute-start(f32[8,64,128]{2,1,0:T(8,128)S(1)} %get-tuple-element.1072), channel_id=1, source_target_pairs={{0,1},{1,2},{2,3},{4,5},{5,6},{6,7},{8,9},{9,10},{10,11},{12,13},{... | collective-permute-start | bytes 786440 | tf_op jit(solution)/shard_map/while/body/eval_jaxpr/ppermute | solution.py:15
  112.7 9.1 %collective-permute-start = (f32[8,64,128]{2,1,0:T(8,128)S(1)}, f32[8,64,128]{2,1,0:T(8,128)S(1)}, u32[]{:S(2)}, u32[]{:S(2)}) collective-permute-start(f32[8,64,128]{2,1,0:T(8,128)S(1)} %get-tuple-element.1072), channel_id=1, source_target_pairs={{0,1},{1,2},{2,3},{4,5},{5,6},{6,7},{8,9},{9,10},{10,11},{12,13},{... | collective-permute-start | bytes 786440 | tf_op jit(solution)/shard_map/while/body/eval_jaxpr/ppermute | solution.py:15
  123.4 14.9 %collective-permute-start = (f32[8,64,128]{2,1,0:T(8,128)S(1)}, f32[8,64,128]{2,1,0:T(8,128)S(1)}, u32[]{:S(2)}, u32[]{:S(2)}) collective-permute-start(f32[8,64,128]{2,1,0:T(8,128)S(1)} %get-tuple-element.1072), channel_id=1, source_target_pairs={{0,1},{1,2},{2,3},{4,5},{5,6},{6,7},{8,9},{9,10},{10,11},{12,13},{... | collective-permute-start | bytes 786440 | tf_op jit(solution)/shard_map/while/body/eval_jaxpr/ppermute | solution.py:15
  152.8 5.2 %collective-permute-start.1 = (f32[8,64,128]{2,1,0:T(8,128)S(1)}, f32[8,64,128]{2,1,0:T(8,128)S(1)}, u32[]{:S(2)}, u32[]{:S(2)}) collective-permute-start(f32[8,64,128]{2,1,0:T(8,128)S(1)} %get-tuple-element.1091), channel_id=1, source_target_pairs={{0,1},{1,2},{2,3},{4,5},{5,6},{6,7},{8,9},{9,10},{10,11},{12,13},{... | collective-permute-start | bytes 786440 | tf_op jit(solution)/shard_map/while/body/eval_jaxpr/ppermute | solution.py:15
  164.5 9.5 %collective-permute-start.1 = (f32[8,64,128]{2,1,0:T(8,128)S(1)}, f32[8,64,128]{2,1,0:T(8,128)S(1)}, u32[]{:S(2)}, u32[]{:S(2)}) collective-permute-start(f32[8,64,128]{2,1,0:T(8,128)S(1)} %get-tuple-element.1091), channel_id=1, source_target_pairs={{0,1},{1,2},{2,3},{4,5},{5,6},{6,7},{8,9},{9,10},{10,11},{12,13},{... | collective-permute-start | bytes 786440 | tf_op jit(solution)/shard_map/while/body/eval_jaxpr/ppermute | solution.py:15
  180.6 8.3 %collective-permute-start.1 = (f32[8,64,128]{2,1,0:T(8,128)S(1)}, f32[8,64,128]{2,1,0:T(8,128)S(1)}, u32[]{:S(2)}, u32[]{:S(2)}) collective-permute-start(f32[8,64,128]{2,1,0:T(8,128)S(1)} %get-tuple-element.1091), channel_id=1, source_target_pairs={{0,1},{1,2},{2,3},{4,5},{5,6},{6,7},{8,9},{9,10},{10,11},{12,13},{... | collective-permute-start | bytes 786440 | tf_op jit(solution)/shard_map/while/body/eval_jaxpr/ppermute | solution.py:15
  195.5 8.3 %collective-permute-start.1 = (f32[8,64,128]{2,1,0:T(8,128)S(1)}, f32[8,64,128]{2,1,0:T(8,128)S(1)}, u32[]{:S(2)}, u32[]{:S(2)}) collective-permute-start(f32[8,64,128]{2,1,0:T(8,128)S(1)} %get-tuple-element.1091), channel_id=1, source_target_pairs={{0,1},{1,2},{2,3},{4,5},{5,6},{6,7},{8,9},{9,10},{10,11},{12,13},{... | collective-permute-start | bytes 786440 | tf_op jit(solution)/shard_map/while/body/eval_jaxpr/ppermute | solution.py:15
  205.2 15.0 %collective-permute-start.1 = (f32[8,64,128]{2,1,0:T(8,128)S(1)}, f32[8,64,128]{2,1,0:T(8,128)S(1)}, u32[]{:S(2)}, u32[]{:S(2)}) collective-permute-start(f32[8,64,128]{2,1,0:T(8,128)S(1)} %get-tuple-element.1091), channel_id=1, source_target_pairs={{0,1},{1,2},{2,3},{4,5},{5,6},{6,7},{8,9},{9,10},{10,11},{12,13},{... | collective-permute-start | bytes 786440 | tf_op jit(solution)/shard_map/while/body/eval_jaxpr/ppermute | solution.py:15
  221.7 9.1 %collective-permute-start.1 = (f32[8,64,128]{2,1,0:T(8,128)S(1)}, f32[8,64,128]{2,1,0:T(8,128)S(1)}, u32[]{:S(2)}, u32[]{:S(2)}) collective-permute-start(f32[8,64,128]{2,1,0:T(8,128)S(1)} %get-tuple-element.1091), channel_id=1, source_target_pairs={{0,1},{1,2},{2,3},{4,5},{5,6},{6,7},{8,9},{9,10},{10,11},{12,13},{... | collective-permute-start | bytes 786440 | tf_op jit(solution)/shard_map/while/body/eval_jaxpr/ppermute | solution.py:15
  232.2 12.9 %collective-permute-start.1 = (f32[8,64,128]{2,1,0:T(8,128)S(1)}, f32[8,64,128]{2,1,0:T(8,128)S(1)}, u32[]{:S(2)}, u32[]{:S(2)}) collective-permute-start(f32[8,64,128]{2,1,0:T(8,128)S(1)} %get-tuple-element.1091), channel_id=1, source_target_pairs={{0,1},{1,2},{2,3},{4,5},{5,6},{6,7},{8,9},{9,10},{10,11},{12,13},{... | collective-permute-start | bytes 786440 | tf_op jit(solution)/shard_map/while/body/eval_jaxpr/ppermute | solution.py:15
  245.2 6.3 %copy-start.7 = (s32[512]{0:T(512)S(1)}, s32[512]{0:T(512)}, u32[]{:S(2)}) copy-start(s32[512]{0:T(512)} %compare_select_fusion) | copy-start | bytes 6148
  245.2 15.4 %copy-start.9 = (f32[2,512]{1,0:T(2,128)S(1)}, f32[2,512]{1,0:T(2,128)}, u32[]{:S(2)}) copy-start(f32[2,512]{1,0:T(2,128)} %param.28) | copy-start | bytes 12292
  245.2 15.4 %copy-start.10 = (pred[512]{0:T(512)(128)(4,1)S(1)}, pred[512]{0:T(512)(128)(4,1)}, u32[]{:S(2)}) copy-start(pred[512]{0:T(512)(128)(4,1)} %compare_and_fusion) | copy-start | bytes 1540
  251.4 9.2 %copy-start.4 = (f32[32,2,512]{2,1,0:T(2,128)S(1)}, f32[32,2,512]{2,1,0:T(2,128)}, u32[]{:S(2)}) copy-start(f32[32,2,512]{2,1,0:T(2,128)} %param.29) | copy-start | bytes 393220
  251.4 9.2 %copy-start.8 = (f32[2,512]{1,0:T(2,128)S(1)}, f32[2,512]{1,0:T(2,128)}, u32[]{:S(2)}) copy-start(f32[2,512]{1,0:T(2,128)} %param.27) | copy-start | bytes 12292
  275.7 49.6 %all-gather.6.cloned.1.call-start = ((), (), s32[]{:S(2)}) async-start(), calls=%async_computation.1 | async-start | bytes 1179648 | tf_op jit(solution)/shard_map/all_gather | solution.py:185
  276.4 72.3 %all-gather.8.cloned.1.call-start = ((), (), s32[]{:S(2)}) async-start(), calls=%async_computation.2 | async-start | bytes 1179648 | tf_op jit(solution)/shard_map/all_gather | solution.py:198
  277.1 119.5 %all-reduce.4.cloned.1.call-start = ((), (), s32[]{:S(2)}) async-start(), calls=%async_computation.3 | async-start | bytes 1048576 | tf_op jit(solution)/shard_map/psum | solution.py:195
  301.2 24.1 %copy-start = (f32[256,2,512]{2,0,1:T(8,128)S(1)}, f32[256,2,512]{2,0,1:T(8,128)}, u32[]{:S(2)}) copy-start(f32[256,2,512]{2,0,1:T(8,128)} %all-gather.4.cloned.1.call-done) | copy-start | bytes 3145732
  397.6 60.8 %copy-start.3 = (f32[256,256]{1,0:T(8,128)S(1)}, f32[256,256]{1,0:T(8,128)}, u32[]{:S(2)}) copy-start(f32[256,256]{1,0:T(8,128)} %get-tuple-element.810) | copy-start | bytes 786436
  420.3 39.9 %copy-start.2 = (f32[32,8,128]{2,1,0:T(8,128)S(1)}, f32[32,8,128]{2,1,0:T(8,128)}, u32[]{:S(2)}) copy-start(f32[32,8,128]{2,1,0:T(8,128)} %param.20) | copy-start | bytes 393220
Sparse Core Ops, SparseCore 0:
  275.8 25.3 all-gather.3
  303.4 21.8 all-gather.5
  326.8 21.8 all-gather.7
  351.5 45.0 all-reduce.3
where the time goes:
time: 471 us; the launch traced here: 468 us
  waiting for transfers between devices  172 us (37%)
  other arithmetic  102 us (22%)
  starting transfers between devices  80.2 us (17%)
  local copies, waits for them, and re-layouts  56.3 us (12%)
  matrix products  27.6 us (6%)
  between operations  15.4 us (3%)
  blocking collectives  13.6 us (3%)
    ppermute x14, starting transfers between devices, shifted(): return lax.ppermute(block, axis, route)  79.8 us
    ppermute x14, waiting for transfers between devices, shifted(): return lax.ppermute(block, axis, route)  61.7 us
    psum x1, waiting for transfers between devices, shards(): gram_matrix, cross_matrix = lax.psum((gram_part, cross_part), 'basin')  45.1 us
    another operation x6, other arithmetic, solve_gram(): factor = jnp.linalg.cholesky(gram_matrix)  34.1 us
    all_gather x1, waiting for transfers between devices, shards(): lax.all_gather(scaled, 'member', axis=0, tiled=True)  23.8 us
    all_gather x1, waiting for transfers between devices, shards(): lax.all_gather(innovation, 'member', axis=0, tiled=True)  20.7 us
    another operation x3, other arithmetic, solve_gram(): lax.linalg.triangular_solve(factor, halfway, left_side=True, lower=True,...  19.7 us
    all_gather x1, waiting for transfers between devices, shards(): prior_all = lax.all_gather(prior_params, 'member', axis=0, tiled=True)  19.7 us
  transfers between devices with their start and end apart: 18, of which 18 were waited for; matrix products, arithmetic and copies ran while one was open for 2% of the time, Pallas kernels for 0%

commit v1 on v0

--- a/solution.py
+++ b/solution.py
@@ -7,6 +7,28 @@
 LANES = 128
 BLK_LEV = 64
 exact_mode = lax.Precision.HIGHEST
+
+
+def joined_along(blocks, dim):
+    shape = list(blocks.shape[1:])
+    shape[dim] *= blocks.shape[0]
+    return jnp.moveaxis(blocks, 0, dim).reshape(shape)
+
+
+def collected_by_bits(x, axis):
+    devices = lax.axis_size(axis)
+    blocks = x[None]
+    for level in range(devices.bit_length() - 1):
+        bit = 1 << level
+        other = lax.ppermute(blocks, axis, [(i, i ^ bit) for i in range(devices)])
+        both = jnp.stack([blocks, other])
+        upper = lax.axis_index(axis) >> level & 1
+        blocks = jnp.where(upper == 0, both, both[::-1]).reshape(-1, *x.shape)
+    return blocks
+
+
+def doubled_up(value, axis, dim):
+    return joined_along(collected_by_bits(value, axis), dim)
 
 
 def shifted(block, axis, distance):
@@ -181,7 +203,7 @@
     mean_pred = lax.psum(jnp.sum(predicted, 0), "member") / members
     scaled = (predicted - mean_pred) / (spread_root * (2.0 * spread))
     scaled_all, innov_all = (
-        lax.all_gather(scaled, "member", axis=0, tiled=True),
+        doubled_up(scaled, "member", 0),
         lax.all_gather(innovation, "member", axis=0, tiled=True),
     )
     scaled_rows = scaled_all.reshape(members, -1)

time: 471 us -> 453 us (0.962)
  waiting for transfers between devices: 172 us -> 155 us
    ppermute x0 -> x3, waiting for transfers between devices: none -> 48.7 us  [collected_by_bits(): other = lax.ppermute(blocks, axis, [(i, i ^ bit) for i in range(devices)])]
    all_gather x1 -> x0, waiting for transfers between devices: 23.8 us -> none  [shards(): lax.all_gather(scaled, 'member', axis=0, tiled=True)]
    all_gather x1, waiting for transfers between devices: 20.7 us -> 0.01 us  [shards(): lax.all_gather(innovation, 'member', axis=0, tiled=True)]
    all_gather x1, waiting for transfers between devices: 19.7 us -> 0.01 us  [shards(): prior_all = lax.all_gather(prior_params, 'member', axis=0, tiled=True)]
  transfers between devices with their start and end apart: 18 -> 20, of which waited for: 18 -> 18; matrix products, arithmetic and copies ran while one was open for 2% -> 2% of each run, Pallas kernels for 0% -> 0%
where the time goes in v1:
time: 453 us; the launch traced here: 451 us
  waiting for transfers between devices  155 us (34%)
  other arithmetic  101 us (22%)
  starting transfers between devices  80.4 us (18%)
  local copies, waits for them, and re-layouts  59.4 us (13%)
  matrix products  24.7 us (5%)
  between operations  15.5 us (3%)
  blocking collectives  13.6 us (3%)
    ppermute x14, starting transfers between devices, shifted(): return lax.ppermute(block, axis, route)  79.8 us
    ppermute x14, waiting for transfers between devices, shifted(): return lax.ppermute(block, axis, route)  61.7 us
    ppermute x3, waiting for transfers between devices, collected_by_bits(): other = lax.ppermute(blocks, axis, [(i, i ^ bit) for i in range(devices)])  48.7 us
    psum x1, waiting for transfers between devices, shards(): gram_matrix, cross_matrix = lax.psum((gram_part, cross_part), 'basin')  44.3 us
    another operation x6, other arithmetic, solve_gram(): factor = jnp.linalg.cholesky(gram_matrix)  34.2 us
    another operation x3, other arithmetic, solve_gram(): lax.linalg.triangular_solve(factor, halfway, left_side=True, lower=True,...  19.7 us
    dot_general x16, matrix products, level_sweep(): jnp.einsum('nj,gjr->gnr', one_hot[level_idx], outflow, precision=exact_mode)  14.7 us
    psum x1, blocking collectives, shards(): mean_pred = lax.psum(jnp.sum(predicted, 0), 'member') / members  13.6 us
  transfers between devices with their start and end apart: 20, of which 18 were waited for; matrix products, arithmetic and copies ran while one was open for 2% of the time, Pallas kernels for 0%

profile of v1, /device:TPU:0, one launch (start us, length us, event | category | flops | bytes accessed | tf_op | source)
XLA Modules:
  0.0 451.1 jit_solution(17639809582739261375)
XLA Ops:
  12.6 6.6 %reshape.353 = f32[32,2,128,128]{3,2,1,0:T(8,128)} reshape(f32[32,2,16384]{2,1,0:T(2,128)} %param.21) | data formatting | bytes 8388608 | tf_op jit(solution)/shard_map/reshape | solution.py:174
  19.2 4.9 %slice_bitcast_fusion.13 = (f32[32,128,128]{2,1,0:T(8,128)}, f32[32,128,128]{2,1,0:T(8,128)}) fusion(f32[32,2,128,128]{3,2,1,0:T(8,128)} %reshape.353), kind=kLoop, calls=%fused_computation.78 | loop fusion | bytes 8388608 | tf_op jit(solution)/shard_map/squeeze | solution.py:185
  24.1 3.5 convolution_exponential_fusion
  28.3 1.6 broadcast.394.clone
  30.0 1.5 broadcast.394.clone.1
  31.5 106.7 %while.39 = (s32[]{:T(128)}, f32[8,64,128]{2,1,0:T(8,128)S(1)}, f32[32,128,128]{2,1,0:T(8,128)}, f32[32,128,128]{2,1,0:T(8,128)}, s32[]{:T(128)}, /*index=5*/f32...) while((s32[]{:T(128)}, f32[8,64,128]{2,1,0:T(8,128)S(1)}, ...), condition=%wide.region_3.4_spmd.clone, body=%wide.region_0.3_spmd.clone.sunk | while | flops 102023184 | bytes 7075321 | solution.py:140
  33.0 5.8 %conditional.6 = (f32[8,64,128]{2,1,0:T(8,128)S(1)}, f32[32,128,128]{2,1,0:T(8,128)}, f32[32,128,128]{2,1,0:T(8,128)}) conditional(s32[]{:T(128)} %convert_element_type.73, (f32[32,128,128]{2,1,0:T(8,128)}, f32[32,128,128]{2,1,0:T(8,128)}) %tuple.159, (s32[]{:T(128)}, f32[32,128,1]{1,0,2:T(8,128)S(1)}, f32[128,128]{1,0:T(8,128)S(1)}, ...), branch_computations={%region_1.1_spmd, %region_2.2_spmd} | conditional | flops 101974024 | bytes 5927046 | solution.py:130
  40.1 6.5 %collective-permute-done = f32[8,64,128]{2,1,0:T(8,128)S(1)} collective-permute-done((f32[8,64,128]{2,1,0:T(8,128)S(1)}, f32[8,64,128]{2,1,0:T(8,128)S(1)}, u32[]{:S(2)}, u32[]{:S(2)}) %collective-permute-start) | collective-permute-done | bytes 262176 | tf_op jit(solution)/shard_map/while/body/eval_jaxpr/ppermute | solution.py:37
  47.9 5.7 %conditional.6 = (f32[8,64,128]{2,1,0:T(8,128)S(1)}, f32[32,128,128]{2,1,0:T(8,128)}, f32[32,128,128]{2,1,0:T(8,128)}) conditional(s32[]{:T(128)} %convert_element_type.73, (f32[32,128,128]{2,1,0:T(8,128)}, f32[32,128,128]{2,1,0:T(8,128)}) %tuple.159, (s32[]{:T(128)}, f32[32,128,1]{1,0,2:T(8,128)S(1)}, f32[128,128]{1,0:T(8,128)S(1)}, ...), branch_computations={%region_1.1_spmd, %region_2.2_spmd} | conditional | flops 101974024 | bytes 5927046 | solution.py:130
  50.9 1.4 multiply_add_fusion
  53.7 4.4 collective-permute-start
  58.1 5.6 %collective-permute-done = f32[8,64,128]{2,1,0:T(8,128)S(1)} collective-permute-done((f32[8,64,128]{2,1,0:T(8,128)S(1)}, f32[8,64,128]{2,1,0:T(8,128)S(1)}, u32[]{:S(2)}, u32[]{:S(2)}) %collective-permute-start) | collective-permute-done | bytes 262176 | tf_op jit(solution)/shard_map/while/body/eval_jaxpr/ppermute | solution.py:37
  65.2 5.8 %conditional.6 = (f32[8,64,128]{2,1,0:T(8,128)S(1)}, f32[32,128,128]{2,1,0:T(8,128)}, f32[32,128,128]{2,1,0:T(8,128)}) conditional(s32[]{:T(128)} %convert_element_type.73, (f32[32,128,128]{2,1,0:T(8,128)}, f32[32,128,128]{2,1,0:T(8,128)}) %tuple.159, (s32[]{:T(128)}, f32[32,128,1]{1,0,2:T(8,128)S(1)}, f32[128,128]{1,0:T(8,128)S(1)}, ...), branch_computations={%region_1.1_spmd, %region_2.2_spmd} | conditional | flops 101974024 | bytes 5927046 | solution.py:130
  70.9 4.4 collective-permute-start
  75.3 4.8 %collective-permute-done = f32[8,64,128]{2,1,0:T(8,128)S(1)} collective-permute-done((f32[8,64,128]{2,1,0:T(8,128)S(1)}, f32[8,64,128]{2,1,0:T(8,128)S(1)}, u32[]{:S(2)}, u32[]{:S(2)}) %collective-permute-start) | collective-permute-done | bytes 262176 | tf_op jit(solution)/shard_map/while/body/eval_jaxpr/ppermute | solution.py:37
  81.5 5.8 %conditional.6 = (f32[8,64,128]{2,1,0:T(8,128)S(1)}, f32[32,128,128]{2,1,0:T(8,128)}, f32[32,128,128]{2,1,0:T(8,128)}) conditional(s32[]{:T(128)} %convert_element_type.73, (f32[32,128,128]{2,1,0:T(8,128)}, f32[32,128,128]{2,1,0:T(8,128)}) %tuple.159, (s32[]{:T(128)}, f32[32,128,1]{1,0,2:T(8,128)S(1)}, f32[128,128]{1,0:T(8,128)S(1)}, ...), branch_computations={%region_1.1_spmd, %region_2.2_spmd} | conditional | flops 101974024 | bytes 5927046 | solution.py:130
  87.3 4.4 collective-permute-start
  91.7 3.9 collective-permute-done
  97.1 10.3 %collective-permute-start = (f32[8,64,128]{2,1,0:T(8,128)S(1)}, f32[8,64,128]{2,1,0:T(8,128)S(1)}, u32[]{:S(2)}, u32[]{:S(2)}) collective-permute-start(f32[8,64,128]{2,1,0:T(8,128)S(1)} %get-tuple-element.1087), channel_id=1, source_target_pairs={{0,1},{1,2},{2,3},{4,5},{5,6},{6,7},{8,9},{9,10},{10,11},{12,13},{... | collective-permute-start | bytes 786440 | tf_op jit(solution)/shard_map/while/body/eval_jaxpr/ppermute | solution.py:37
  107.4 3.9 collective-permute-done
  112.7 5.3 %collective-permute-start = (f32[8,64,128]{2,1,0:T(8,128)S(1)}, f32[8,64,128]{2,1,0:T(8,128)S(1)}, u32[]{:S(2)}, u32[]{:S(2)}) collective-permute-start(f32[8,64,128]{2,1,0:T(8,128)S(1)} %get-tuple-element.1087), channel_id=1, source_target_pairs={{0,1},{1,2},{2,3},{4,5},{5,6},{6,7},{8,9},{9,10},{10,11},{12,13},{... | collective-permute-start | bytes 786440 | tf_op jit(solution)/shard_map/while/body/eval_jaxpr/ppermute | solution.py:37
  118.0 3.9 collective-permute-done
  123.4 11.0 %collective-permute-start = (f32[8,64,128]{2,1,0:T(8,128)S(1)}, f32[8,64,128]{2,1,0:T(8,128)S(1)}, u32[]{:S(2)}, u32[]{:S(2)}) collective-permute-start(f32[8,64,128]{2,1,0:T(8,128)S(1)} %get-tuple-element.1087), channel_id=1, source_target_pairs={{0,1},{1,2},{2,3},{4,5},{5,6},{6,7},{8,9},{9,10},{10,11},{12,13},{... | collective-permute-start | bytes 786440 | tf_op jit(solution)/shard_map/while/body/eval_jaxpr/ppermute | solution.py:37
  134.4 3.9 collective-permute-done
  138.2 6.4 %copy.88 = f32[32,128,128]{0,2,1:T(8,128)} copy(f32[32,128,128]{2,1,0:T(8,128)} %get-tuple-element.1182) | data formatting | bytes 4194304 | tf_op jit(solution)/shard_map/while | solution.py:140
  144.6 1.6 broadcast.394
  146.2 98.9 %while.40 = (s32[]{:T(128)}, f32[8,64,128]{2,1,0:T(8,128)S(1)}, f32[32,128,128]{2,1,0:T(8,128)}, s32[]{:T(128)}, f32[32,128,1]{1,0,2:T(8,128)S(1)}, /*index=5*/f...) while((s32[]{:T(128)}, f32[8,64,128]{2,1,0:T(8,128)S(1)}, ...), condition=%wide.region_7.9_spmd.clone, body=%wide.region_4.8_spmd.clone.sunk | while | flops 101892112 | bytes 6157773 | solution.py:140
  147.7 5.1 %conditional.7 = (f32[8,64,128]{2,1,0:T(8,128)S(1)}, f32[32,128,128]{2,1,0:T(8,128)}) conditional(s32[]{:T(128)} %convert_element_type.76, f32[32,128,128]{2,1,0:T(8,128)} %get-tuple-element.1191, (s32[]{:T(128)}, f32[32,128,1]{1,0,2:T(8,128)S(1)}, f32[128,128]{1,0:T(8,128)S(1)}, f32[32,128,128]{2,1,0:T(8,128)}, f32[32,128,128]{2,1,0:T(8,128)S(1)}, ...), branch_computations={%region_5.6_spmd, %region_6.7_spmd} | conditional | flops 101842952 | bytes 5009530 | solution.py:130
  150.0 1.6 fusion.26
  154.1 3.9 collective-permute-done.1
  159.4 5.2 %conditional.7 = (f32[8,64,128]{2,1,0:T(8,128)S(1)}, f32[32,128,128]{2,1,0:T(8,128)}) conditional(s32[]{:T(128)} %convert_element_type.76, f32[32,128,128]{2,1,0:T(8,128)} %get-tuple-element.1191, (s32[]{:T(128)}, f32[32,128,1]{1,0,2:T(8,128)S(1)}, f32[128,128]{1,0:T(8,128)S(1)}, f32[32,128,128]{2,1,0:T(8,128)}, f32[32,128,128]{2,1,0:T(8,128)S(1)}, ...), branch_computations={%region_5.6_spmd, %region_6.7_spmd} | conditional | flops 101842952 | bytes 5009530 | solution.py:130
  161.8 1.6 fusion.26
  164.6 5.6 %collective-permute-start.1 = (f32[8,64,128]{2,1,0:T(8,128)S(1)}, f32[8,64,128]{2,1,0:T(8,128)S(1)}, u32[]{:S(2)}, u32[]{:S(2)}) collective-permute-start(f32[8,64,128]{2,1,0:T(8,128)S(1)} %get-tuple-element.1106), channel_id=1, source_target_pairs={{0,1},{1,2},{2,3},{4,5},{5,6},{6,7},{8,9},{9,10},{10,11},{12,13},{... | collective-permute-start | bytes 786440 | tf_op jit(solution)/shard_map/while/body/eval_jaxpr/ppermute | solution.py:37
  170.2 3.9 collective-permute-done.1
  175.5 5.1 %conditional.7 = (f32[8,64,128]{2,1,0:T(8,128)S(1)}, f32[32,128,128]{2,1,0:T(8,128)}) conditional(s32[]{:T(128)} %convert_element_type.76, f32[32,128,128]{2,1,0:T(8,128)} %get-tuple-element.1191, (s32[]{:T(128)}, f32[32,128,1]{1,0,2:T(8,128)S(1)}, f32[128,128]{1,0:T(8,128)S(1)}, f32[32,128,128]{2,1,0:T(8,128)}, f32[32,128,128]{2,1,0:T(8,128)S(1)}, ...), branch_computations={%region_5.6_spmd, %region_6.7_spmd} | conditional | flops 101842952 | bytes 5009530 | solution.py:130
  177.9 1.6 fusion.26
  180.6 4.4 collective-permute-start.1
  185.1 3.9 collective-permute-done.1
  190.3 5.1 %conditional.7 = (f32[8,64,128]{2,1,0:T(8,128)S(1)}, f32[32,128,128]{2,1,0:T(8,128)}) conditional(s32[]{:T(128)} %convert_element_type.76, f32[32,128,128]{2,1,0:T(8,128)} %get-tuple-element.1191, (s32[]{:T(128)}, f32[32,128,1]{1,0,2:T(8,128)S(1)}, f32[128,128]{1,0:T(8,128)S(1)}, f32[32,128,128]{2,1,0:T(8,128)}, f32[32,128,128]{2,1,0:T(8,128)S(1)}, ...), branch_computations={%region_5.6_spmd, %region_6.7_spmd} | conditional | flops 101842952 | bytes 5009530 | solution.py:130
  192.7 1.6 fusion.26
  195.5 4.4 collective-permute-start.1
  199.9 3.9 collective-permute-done.1
  205.2 9.5 %collective-permute-start.1 = (f32[8,64,128]{2,1,0:T(8,128)S(1)}, f32[8,64,128]{2,1,0:T(8,128)S(1)}, u32[]{:S(2)}, u32[]{:S(2)}) collective-permute-start(f32[8,64,128]{2,1,0:T(8,128)S(1)} %get-tuple-element.1106), channel_id=1, source_target_pairs={{0,1},{1,2},{2,3},{4,5},{5,6},{6,7},{8,9},{9,10},{10,11},{12,13},{... | collective-permute-start | bytes 786440 | tf_op jit(solution)/shard_map/while/body/eval_jaxpr/ppermute | solution.py:37
  214.7 5.5 %collective-permute-done.1 = f32[8,64,128]{2,1,0:T(8,128)S(1)} collective-permute-done((f32[8,64,128]{2,1,0:T(8,128)S(1)}, f32[8,64,128]{2,1,0:T(8,128)S(1)}, u32[]{:S(2)}, u32[]{:S(2)}) %collective-permute-start.1) | collective-permute-done | bytes 262176 | tf_op jit(solution)/shard_map/while/body/eval_jaxpr/ppermute | solution.py:37
  221.7 4.4 collective-permute-start.1
  226.1 4.6 %collective-permute-done.1 = f32[8,64,128]{2,1,0:T(8,128)S(1)} collective-permute-done((f32[8,64,128]{2,1,0:T(8,128)S(1)}, f32[8,64,128]{2,1,0:T(8,128)S(1)}, u32[]{:S(2)}, u32[]{:S(2)}) %collective-permute-start.1) | collective-permute-done | bytes 262176 | tf_op jit(solution)/shard_map/while/body/eval_jaxpr/ppermute | solution.py:37
  232.2 9.1 %collective-permute-start.1 = (f32[8,64,128]{2,1,0:T(8,128)S(1)}, f32[8,64,128]{2,1,0:T(8,128)S(1)}, u32[]{:S(2)}, u32[]{:S(2)}) collective-permute-start(f32[8,64,128]{2,1,0:T(8,128)S(1)} %get-tuple-element.1106), channel_id=1, source_target_pairs={{0,1},{1,2},{2,3},{4,5},{5,6},{6,7},{8,9},{9,10},{10,11},{12,13},{... | collective-permute-start | bytes 786440 | tf_op jit(solution)/shard_map/while/body/eval_jaxpr/ppermute | solution.py:37
  241.3 3.9 collective-permute-done.1
  245.2 6.3 %copy.90 = f32[32,128,128]{0,2,1:T(8,128)} copy(f32[32,128,128]{2,1,0:T(8,128)} %get-tuple-element.648) | data formatting | bytes 4194304 | tf_op jit(solution)/shard_map/while | solution.py:140
  251.5 4.4 gather_fusion.1
  256.0 4.4 gather_fusion
  261.6 13.6 %psum.21 = f32[2,512]{1,0:T(2,128)S(1)} all-reduce(f32[2,512]{1,0:T(2,128)S(1)} %get-tuple-element.857), channel_id=1, replica_groups=mesh['member'=8,'basin'=4] {'member'}, use_global_device_ids=true, to_apply=%region_9.11 | all-reduce | flops 1024 | bytes 8192 | tf_op jit(solution)/shard_map/psum | solution.py:203
  277.1 14.8 %collective-permute-done.3 = f32[2,32,2,512]{3,1,2,0:T(8,128)S(1)} collective-permute-done((f32[2,32,2,512]{3,1,2,0:T(8,128)S(1)}, f32[2,32,2,512]{3,1,2,0:T(8,128)S(1)}, u32[]{:S(2)}, u32[]{:S(2)}) %collective-permute-start.3) | collective-permute-done | bytes 262176 | tf_op jit(solution)/shard_map/ppermute | solution.py:23
  292.8 32.6 %collective-permute-done.4 = f32[4,32,2,512]{3,2,1,0:T(2,128)S(1)} collective-permute-done((f32[4,32,2,512]{3,2,1,0:T(2,128)S(1)}, f32[4,32,2,512]{3,2,1,0:T(2,128)S(1)}, u32[]{:S(2)}, u32[]{:S(2)}) %collective-permute-start.4) | collective-permute-done | bytes 524320 | tf_op jit(solution)/shard_map/ppermute | solution.py:23
  326.6 1.7 fusion.107
  328.3 1.4 copy.112
  329.7 1.7 fusion.108
  332.3 1.5 reduce_sum.19
  335.1 44.3 %all-reduce.4.cloned.1.call-done = (f32[256,256]{1,0:T(8,128)}, f32[256,256]{0,1:T(8,128)}) async-done(((f32[256,256]{1,0:T(8,128)}, f32[256,256]{0,1:T(8,128)}), (f32[256,256]{1,0:T(8,128)}, f32[256,256]{0,1:T(8,128)})) %all-reduce.4.cloned.1.call-update) | async-done | bytes 524304 | tf_op jit(solution)/shard_map/psum | solution.py:217
  381.5 11.7 %cholesky.49 = f32[128,128]{1,0:T(8,128)S(1)} custom-call(f32[128,128]{1,0:T(8,128)S(1)} %cholesky.115), custom_call_target="Cholesky" | custom-call | tf_op jit(solution)/shard_map/jit(cholesky)/cholesky | solution.py:65
  393.3 9.8 %custom-call.16 = f32[1,128,128]{1,2,0:T(8,128)S(1)} custom-call(f32[1,128,128]{2,1,0:T(8,128)S(1)} %get-tuple-element.871), custom_call_target="InvertDiagBlocksLowerTriangular" | custom-call | tf_op jit(solution)/shard_map/jit(cholesky)/cholesky | solution.py:65
  403.6 11.9 %cholesky.102 = f32[128,128]{1,0:T(8,128)S(1)} custom-call(f32[128,128]{1,0:T(8,128)S(1)} %convolution_subtract_fusion.2), custom_call_target="Cholesky" | custom-call | tf_op jit(solution)/shard_map/jit(cholesky)/cholesky | solution.py:65
  417.6 3.9 while.38
  421.5 19.7 %custom-call.17 = f32[2,128,128]{1,2,0:T(8,128)S(1)} custom-call(f32[2,128,128]{2,1,0:T(8,128)S(1)} %get-tuple-element.656), custom_call_target="InvertDiagBlocksLowerTriangular" | custom-call | tf_op jit(solution)/shard_map/triangular_solve | solution.py:67
  (221 shorter events, 82.1 us)
Async XLA Ops:
  7.2 321.2 %all-gather.3.cloned.1.call-start = ((), (), s32[]{:S(2)}) async-start(), calls=%async_computation | async-start | bytes 1179648 | tf_op jit(solution)/shard_map/all_gather | solution.py:207
  19.2 4.9 %copy-start = (f32[32,8,128]{2,1,0:T(8,128)S(1)}, f32[32,8,128]{2,1,0:T(8,128)}, u32[]{:S(2)}) copy-start(f32[32,8,128]{2,1,0:T(8,128)} %param.20) | copy-start | bytes 393220
  24.1 3.5 copy-start.4
  24.1 3.5 copy-start.5
  38.7 7.8 %collective-permute-start = (f32[8,64,128]{2,1,0:T(8,128)S(1)}, f32[8,64,128]{2,1,0:T(8,128)S(1)}, u32[]{:S(2)}, u32[]{:S(2)}) collective-permute-start(f32[8,64,128]{2,1,0:T(8,128)S(1)} %get-tuple-element.1087), channel_id=1, source_target_pairs={{0,1},{1,2},{2,3},{4,5},{5,6},{6,7},{8,9},{9,10},{10,11},{12,13},{... | collective-permute-start | bytes 786440 | tf_op jit(solution)/shard_map/while/body/eval_jaxpr/ppermute | solution.py:37
  53.7 10.0 %collective-permute-start = (f32[8,64,128]{2,1,0:T(8,128)S(1)}, f32[8,64,128]{2,1,0:T(8,128)S(1)}, u32[]{:S(2)}, u32[]{:S(2)}) collective-permute-start(f32[8,64,128]{2,1,0:T(8,128)S(1)} %get-tuple-element.1087), channel_id=1, source_target_pairs={{0,1},{1,2},{2,3},{4,5},{5,6},{6,7},{8,9},{9,10},{10,11},{12,13},{... | collective-permute-start | bytes 786440 | tf_op jit(solution)/shard_map/while/body/eval_jaxpr/ppermute | solution.py:37
  70.9 9.2 %collective-permute-start = (f32[8,64,128]{2,1,0:T(8,128)S(1)}, f32[8,64,128]{2,1,0:T(8,128)S(1)}, u32[]{:S(2)}, u32[]{:S(2)}) collective-permute-start(f32[8,64,128]{2,1,0:T(8,128)S(1)} %get-tuple-element.1087), channel_id=1, source_target_pairs={{0,1},{1,2},{2,3},{4,5},{5,6},{6,7},{8,9},{9,10},{10,11},{12,13},{... | collective-permute-start | bytes 786440 | tf_op jit(solution)/shard_map/while/body/eval_jaxpr/ppermute | solution.py:37
  87.3 8.3 %collective-permute-start = (f32[8,64,128]{2,1,0:T(8,128)S(1)}, f32[8,64,128]{2,1,0:T(8,128)S(1)}, u32[]{:S(2)}, u32[]{:S(2)}) collective-permute-start(f32[8,64,128]{2,1,0:T(8,128)S(1)} %get-tuple-element.1087), channel_id=1, source_target_pairs={{0,1},{1,2},{2,3},{4,5},{5,6},{6,7},{8,9},{9,10},{10,11},{12,13},{... | collective-permute-start | bytes 786440 | tf_op jit(solution)/shard_map/while/body/eval_jaxpr/ppermute | solution.py:37
  97.1 14.2 %collective-permute-start = (f32[8,64,128]{2,1,0:T(8,128)S(1)}, f32[8,64,128]{2,1,0:T(8,128)S(1)}, u32[]{:S(2)}, u32[]{:S(2)}) collective-permute-start(f32[8,64,128]{2,1,0:T(8,128)S(1)} %get-tuple-element.1087), channel_id=1, source_target_pairs={{0,1},{1,2},{2,3},{4,5},{5,6},{6,7},{8,9},{9,10},{10,11},{12,13},{... | collective-permute-start | bytes 786440 | tf_op jit(solution)/shard_map/while/body/eval_jaxpr/ppermute | solution.py:37
  112.7 9.1 %collective-permute-start = (f32[8,64,128]{2,1,0:T(8,128)S(1)}, f32[8,64,128]{2,1,0:T(8,128)S(1)}, u32[]{:S(2)}, u32[]{:S(2)}) collective-permute-start(f32[8,64,128]{2,1,0:T(8,128)S(1)} %get-tuple-element.1087), channel_id=1, source_target_pairs={{0,1},{1,2},{2,3},{4,5},{5,6},{6,7},{8,9},{9,10},{10,11},{12,13},{... | collective-permute-start | bytes 786440 | tf_op jit(solution)/shard_map/while/body/eval_jaxpr/ppermute | solution.py:37
  123.4 14.9 %collective-permute-start = (f32[8,64,128]{2,1,0:T(8,128)S(1)}, f32[8,64,128]{2,1,0:T(8,128)S(1)}, u32[]{:S(2)}, u32[]{:S(2)}) collective-permute-start(f32[8,64,128]{2,1,0:T(8,128)S(1)} %get-tuple-element.1087), channel_id=1, source_target_pairs={{0,1},{1,2},{2,3},{4,5},{5,6},{6,7},{8,9},{9,10},{10,11},{12,13},{... | collective-permute-start | bytes 786440 | tf_op jit(solution)/shard_map/while/body/eval_jaxpr/ppermute | solution.py:37
  152.8 5.2 %collective-permute-start.1 = (f32[8,64,128]{2,1,0:T(8,128)S(1)}, f32[8,64,128]{2,1,0:T(8,128)S(1)}, u32[]{:S(2)}, u32[]{:S(2)}) collective-permute-start(f32[8,64,128]{2,1,0:T(8,128)S(1)} %get-tuple-element.1106), channel_id=1, source_target_pairs={{0,1},{1,2},{2,3},{4,5},{5,6},{6,7},{8,9},{9,10},{10,11},{12,13},{... | collective-permute-start | bytes 786440 | tf_op jit(solution)/shard_map/while/body/eval_jaxpr/ppermute | solution.py:37
  164.6 9.5 %collective-permute-start.1 = (f32[8,64,128]{2,1,0:T(8,128)S(1)}, f32[8,64,128]{2,1,0:T(8,128)S(1)}, u32[]{:S(2)}, u32[]{:S(2)}) collective-permute-start(f32[8,64,128]{2,1,0:T(8,128)S(1)} %get-tuple-element.1106), channel_id=1, source_target_pairs={{0,1},{1,2},{2,3},{4,5},{5,6},{6,7},{8,9},{9,10},{10,11},{12,13},{... | collective-permute-start | bytes 786440 | tf_op jit(solution)/shard_map/while/body/eval_jaxpr/ppermute | solution.py:37
  180.6 8.3 %collective-permute-start.1 = (f32[8,64,128]{2,1,0:T(8,128)S(1)}, f32[8,64,128]{2,1,0:T(8,128)S(1)}, u32[]{:S(2)}, u32[]{:S(2)}) collective-permute-start(f32[8,64,128]{2,1,0:T(8,128)S(1)} %get-tuple-element.1106), channel_id=1, source_target_pairs={{0,1},{1,2},{2,3},{4,5},{5,6},{6,7},{8,9},{9,10},{10,11},{12,13},{... | collective-permute-start | bytes 786440 | tf_op jit(solution)/shard_map/while/body/eval_jaxpr/ppermute | solution.py:37
  195.5 8.3 %collective-permute-start.1 = (f32[8,64,128]{2,1,0:T(8,128)S(1)}, f32[8,64,128]{2,1,0:T(8,128)S(1)}, u32[]{:S(2)}, u32[]{:S(2)}) collective-permute-start(f32[8,64,128]{2,1,0:T(8,128)S(1)} %get-tuple-element.1106), channel_id=1, source_target_pairs={{0,1},{1,2},{2,3},{4,5},{5,6},{6,7},{8,9},{9,10},{10,11},{12,13},{... | collective-permute-start | bytes 786440 | tf_op jit(solution)/shard_map/while/body/eval_jaxpr/ppermute | solution.py:37
  205.2 15.0 %collective-permute-start.1 = (f32[8,64,128]{2,1,0:T(8,128)S(1)}, f32[8,64,128]{2,1,0:T(8,128)S(1)}, u32[]{:S(2)}, u32[]{:S(2)}) collective-permute-start(f32[8,64,128]{2,1,0:T(8,128)S(1)} %get-tuple-element.1106), channel_id=1, source_target_pairs={{0,1},{1,2},{2,3},{4,5},{5,6},{6,7},{8,9},{9,10},{10,11},{12,13},{... | collective-permute-start | bytes 786440 | tf_op jit(solution)/shard_map/while/body/eval_jaxpr/ppermute | solution.py:37
  221.7 9.0 %collective-permute-start.1 = (f32[8,64,128]{2,1,0:T(8,128)S(1)}, f32[8,64,128]{2,1,0:T(8,128)S(1)}, u32[]{:S(2)}, u32[]{:S(2)}) collective-permute-start(f32[8,64,128]{2,1,0:T(8,128)S(1)} %get-tuple-element.1106), channel_id=1, source_target_pairs={{0,1},{1,2},{2,3},{4,5},{5,6},{6,7},{8,9},{9,10},{10,11},{12,13},{... | collective-permute-start | bytes 786440 | tf_op jit(solution)/shard_map/while/body/eval_jaxpr/ppermute | solution.py:37
  232.2 12.9 %collective-permute-start.1 = (f32[8,64,128]{2,1,0:T(8,128)S(1)}, f32[8,64,128]{2,1,0:T(8,128)S(1)}, u32[]{:S(2)}, u32[]{:S(2)}) collective-permute-start(f32[8,64,128]{2,1,0:T(8,128)S(1)} %get-tuple-element.1106), channel_id=1, source_target_pairs={{0,1},{1,2},{2,3},{4,5},{5,6},{6,7},{8,9},{9,10},{10,11},{12,13},{... | collective-permute-start | bytes 786440 | tf_op jit(solution)/shard_map/while/body/eval_jaxpr/ppermute | solution.py:37
  245.2 6.3 %copy-start.6 = (s32[512]{0:T(512)S(1)}, s32[512]{0:T(512)}, u32[]{:S(2)}) copy-start(s32[512]{0:T(512)} %compare_select_fusion) | copy-start | bytes 6148
  245.2 15.4 %copy-start.8 = (f32[2,512]{1,0:T(2,128)S(1)}, f32[2,512]{1,0:T(2,128)}, u32[]{:S(2)}) copy-start(f32[2,512]{1,0:T(2,128)} %param.28) | copy-start | bytes 12292
  245.2 15.4 %copy-start.9 = (pred[512]{0:T(512)(128)(4,1)S(1)}, pred[512]{0:T(512)(128)(4,1)}, u32[]{:S(2)}) copy-start(pred[512]{0:T(512)(128)(4,1)} %compare_and_fusion) | copy-start | bytes 1540
  251.5 9.2 %copy-start.3 = (f32[32,2,512]{2,1,0:T(2,128)S(1)}, f32[32,2,512]{2,1,0:T(2,128)}, u32[]{:S(2)}) copy-start(f32[32,2,512]{2,1,0:T(2,128)} %param.29) | copy-start | bytes 393220
  251.5 9.2 %copy-start.7 = (f32[2,512]{1,0:T(2,128)S(1)}, f32[2,512]{1,0:T(2,128)}, u32[]{:S(2)}) copy-start(f32[2,512]{1,0:T(2,128)} %param.27) | copy-start | bytes 12292
  261.5 70.7 %all-gather.5.cloned.1.call-start = ((), (), s32[]{:S(2)}) async-start(), calls=%async_computation.1 | async-start | bytes 1179648 | tf_op jit(solution)/shard_map/all_gather | solution.py:220
  275.2 1.4 collective-permute-start.2
  276.7 15.1 %collective-permute-start.3 = (f32[2,32,2,512]{3,1,2,0:T(8,128)S(1)}, f32[2,32,2,512]{3,1,2,0:T(8,128)S(1)}, u32[]{:S(2)}, u32[]{:S(2)}) collective-permute-start(f32[2,32,2,512]{3,1,2,0:T(8,128)S(1)} %get-tuple-element.855), channel_id=1, source_target_pairs={{0,8},{4,12},{8,0},{12,4},{16,24},{20,28},{24,16},{28,20},{1,9},{5... | collective-permute-start | bytes 786440 | tf_op jit(solution)/shard_map/ppermute | solution.py:23
  276.8 102.5 %all-reduce.4.cloned.1.call-start = ((), (), s32[]{:S(2)}) async-start(), calls=%async_computation.2 | async-start | bytes 1048576 | tf_op jit(solution)/shard_map/psum | solution.py:217
  292.3 33.1 %collective-permute-start.4 = (f32[4,32,2,512]{3,2,1,0:T(2,128)S(1)}, f32[4,32,2,512]{3,2,1,0:T(2,128)S(1)}, u32[]{:S(2)}, u32[]{:S(2)}) collective-permute-start(f32[4,32,2,512]{3,2,1,0:T(2,128)S(1)} %copy.94), channel_id=1, source_target_pairs={{0,16},{4,20},{8,24},{12,28},{16,0},{20,4},{24,8},{28,12},{1,17},{... | collective-permute-start | bytes 1572872 | tf_op jit(solution)/shard_map/ppermute | solution.py:23
  380.3 60.8 %copy-start.2 = (f32[256,256]{1,0:T(8,128)S(1)}, f32[256,256]{1,0:T(8,128)}, u32[]{:S(2)}) copy-start(f32[256,256]{1,0:T(8,128)} %get-tuple-element.816) | copy-start | bytes 786436
  403.1 39.9 %copy-start.1 = (f32[32,8,128]{2,1,0:T(8,128)S(1)}, f32[32,8,128]{2,1,0:T(8,128)}, u32[]{:S(2)}) copy-start(f32[32,8,128]{2,1,0:T(8,128)} %param.20) | copy-start | bytes 393220
Sparse Core Ops, SparseCore 0:
  261.7 31.9 all-gather.2
  295.2 25.1 all-gather.4
  331.6 47.6 all-reduce.3
